TPU v7x, 32 devices: a whole 2x2x4 slice. The times are simulated.
32 devices in a mesh: view: 2 (over core), seq: 16 (over z, y, x).
Axes of the slice: x: 2, y: 2, z: 4, core: 2. Of those that a mesh axis runs over, the one named last changes fastest.
Arguments:
- query: bfloat16 [2, 12288, 2560], P('view', 'seq'), may hold values from -60 to 60
- keys: bfloat16 [2, 12288, 2560], P('view', 'seq'), may hold values from -6 to 6
- values: bfloat16 [2, 12288, 2560], P('view', 'seq'), may hold values from -6 to 6
- block_list: int32 [2, 16, 4], P('view', 'seq'), may hold values from 0 to 5, as said below
- block_count: int32 [2, 16], P('view', 'seq'), may hold values from 1 to 4, as said below
Outputs:
- attended: bfloat16 [2, 12288, 2560], P('view', 'seq')
Inputs may be any that keep to these rules, and one draw needn't show every extreme that they name: `block_list`: in each row the first block_count entries are distinct key block indices; later entries are valid indices too. `block_count`: some eye and band uses all 4 entries.
All inputs are finite; a program needn't handle non-finite values.
Results may differ from a plain program's by a relative error of at most 0.0042.
Values may be sent and summed in bfloat16 or wider, within the bound.
A program may use at most 128 MiB of HBM per device.

v0:
```python
import jax
import jax.numpy as jnp
from jax import lax
from jax.sharding import PartitionSpec as P

HEADS = 20
HD = 128
KBLK = 128


def from_partner(x, axis, apart):
    return lax.ppermute(x, axis, [(i, i ^ 1 << apart) for i in range(lax.axis_size(axis))])


def shortened(x):

    def short(part):
        return part.astype(jnp.bfloat16) if part.dtype == jnp.float32 else part

    return jax.tree.map(short, x)


def attend(query, near_k, near_v, far_k, far_v, far_live):
    keys = jnp.concatenate((near_k, far_k), 0)
    vals = jnp.concatenate((near_v, far_v), 0)
    live = jnp.concatenate((jnp.ones((near_k.shape[0],), dtype=bool), far_live), 0)
    scale = HD ** (-0.5)

    def one_head(head):
        start = head * HD
        qpart = lax.dynamic_slice_in_dim(query, start, HD, 1)
        kpart = lax.dynamic_slice_in_dim(keys, start, HD, 1)
        vpart = lax.dynamic_slice_in_dim(vals, start, HD, 1)
        score = (
            lax.dot_general(
                qpart, kpart, (((1,), (1,)), ((), ())), preferred_element_type=jnp.float32
            )
            * scale
        )
        score = jnp.where(live[None, :], score, -1e30)
        top = jnp.max(score, axis=1, keepdims=True)
        weight = jnp.exp(score - top)
        total = jnp.sum(weight, axis=1, keepdims=True)
        mixed = (
            jnp.dot(weight.astype(jnp.bfloat16), vpart, preferred_element_type=jnp.float32) / total
        )
        return mixed.astype(jnp.bfloat16)

    outs = lax.map(one_head, jnp.arange(HEADS, dtype=jnp.int32))
    return jnp.transpose(outs, (1, 0, 2)).reshape(query.shape[0], HEADS * HD)


def block_mask(listed, count, blocks, width):
    slots = jnp.arange(listed.shape[0], dtype=jnp.int32)
    hits = (listed[:, None] == jnp.arange(blocks, dtype=jnp.int32)[None, :]) & (slots < count)[
        :, None
    ]
    return jnp.repeat(jnp.any(hits, axis=0), width, total_repeat_length=blocks * width)


def per_device(query, keys, values, block_list, block_count):
    tokens_here = query.shape[1]
    feat = query.shape[2]
    bands = lax.axis_size("seq")
    cells = tokens_here // bands
    shape_band = (bands, cells, feat)
    paired = jnp.stack((keys[0], values[0]))
    other = from_partner(paired, "view", 0)
    moved = (
        lax.all_to_all(
            query[0].reshape(shape_band), "seq", split_axis=0, concat_axis=0, tiled=True
        ),
        lax.all_to_all(keys[0].reshape(shape_band), "seq", split_axis=0, concat_axis=0, tiled=True),
        lax.all_to_all(
            values[0].reshape(shape_band), "seq", split_axis=0, concat_axis=0, tiled=True
        ),
        lax.all_to_all(
            other[0].reshape(shape_band), "seq", split_axis=0, concat_axis=0, tiled=True
        ),
        lax.all_to_all(
            other[1].reshape(shape_band), "seq", split_axis=0, concat_axis=0, tiled=True
        ),
    )
    band_q = moved[0].reshape(tokens_here, feat)
    band_k = moved[1].reshape(tokens_here, feat)
    band_v = moved[2].reshape(tokens_here, feat)
    far_k = moved[3].reshape(tokens_here, feat)
    far_v = moved[4].reshape(tokens_here, feat)
    listed = block_list[0, 0]
    count = block_count[0, 0]
    blocks = tokens_here // KBLK
    far_live = block_mask(listed, count, blocks, KBLK)
    mixed = attend(band_q, band_k, band_v, far_k, far_v, far_live)
    back = lax.all_to_all(
        shortened(mixed.reshape(shape_band)), "seq", split_axis=0, concat_axis=0, tiled=True
    )
    return back.reshape(1, tokens_here, feat)


def solution(mesh):
    in_specs = (
        P("view", "seq", None),
        P("view", "seq", None),
        P("view", "seq", None),
        P("view", "seq", None),
        P("view", "seq"),
    )
    out_specs = P("view", "seq", None)
    return jax.shard_map(
        per_device, mesh=mesh, in_specs=in_specs, out_specs=out_specs, check_vma=False
    )
```

profile of v0, /device:TPU:0, one launch (start us, length us, event | category | flops | bytes accessed | tf_op | source)
XLA Modules:
  0.0 717.1 jit_solution(7948892887079226849)
XLA Ops:
  0.0 8.4 %all-to-all-start.1 = ((bf16[16,48,2560]{2,1,0:T(8,128)(2,1)}), bf16[16,48,2560]{2,1,0:T(8,128)(2,1)}, u32[]{:S(2)}, u32[]{:S(2)}) async-start(bf16[16,48,2560]{2,1,0:T(8,128)(2,1)} %bitcast.69), calls=%async_computation.1 | async-start | bytes 7864320 | tf_op jit(solution)/shard_map/all_to_all | solution.py:73
  8.4 7.2 %pad_maximum_fusion = bf16[2,768,2560]{2,1,0:T(8,128)(2,1)} fusion(bf16[1,768,2560]{2,1,0:T(8,128)(2,1)} %param.11, bf16[1,768,2560]{2,1,0:T(8,128)(2,1)} %param.10), kind=kLoop, calls=%fused_computation.19 | loop fusion | flops 3932160 | bytes 15728640 | tf_op jit(solution)/shard_map/stack | solution.py:67
  15.6 67.7 %all-to-all-done.1 = bf16[16,48,2560]{2,1,0:T(8,128)(2,1)} async-done(((bf16[16,48,2560]{2,1,0:T(8,128)(2,1)}), bf16[16,48,2560]{2,1,0:T(8,128)(2,1)}, u32[]{:S(2)}, u32[]{:S(2)}) %all-to-all-start.1) | async-done | bytes 3932192 | tf_op jit(solution)/shard_map/all_to_all | solution.py:73
  83.3 19.1 %all-to-all-start.3 = ((bf16[16,48,2560]{2,1,0:T(8,128)(2,1)}), bf16[16,48,2560]{2,1,0:T(8,128)(2,1)}, u32[]{:S(2)}, u32[]{:S(2)}) async-start(bf16[16,48,2560]{2,1,0:T(8,128)(2,1)} %bitcast.70), calls=%async_computation.3 | async-start | bytes 7864320 | tf_op jit(solution)/shard_map/all_to_all | solution.py:74
  102.4 5.6 fusion.36
  108.0 68.3 %all-to-all-done.3 = bf16[16,48,2560]{2,1,0:T(8,128)(2,1)} async-done(((bf16[16,48,2560]{2,1,0:T(8,128)(2,1)}), bf16[16,48,2560]{2,1,0:T(8,128)(2,1)}, u32[]{:S(2)}, u32[]{:S(2)}) %all-to-all-start.3) | async-done | bytes 3932192 | tf_op jit(solution)/shard_map/all_to_all | solution.py:74
  176.3 106.7 %all_to_all.30 = bf16[16,48,2560]{2,1,0:T(8,128)(2,1)} all-to-all(bf16[16,48,2560]{2,1,0:T(8,128)(2,1)} %bitcast.74), channel_id=1, replica_groups=mesh['view'=2,'seq'=16] {'seq'}, dimensions={0} | all-to-all | bytes 7864320 | tf_op jit(solution)/shard_map/all_to_all | solution.py:77
  283.0 91.6 %all_to_all.31 = bf16[16,48,2560]{2,1,0:T(8,128)(2,1)} all-to-all(bf16[16,48,2560]{2,1,0:T(8,128)(2,1)S(1)} %bitcast.73), channel_id=1, replica_groups=mesh['view'=2,'seq'=16] {'seq'}, dimensions={0} | all-to-all | bytes 7864320 | tf_op jit(solution)/shard_map/all_to_all | solution.py:80
  374.6 4.7 all-to-all-start
  380.7 3.6 select_reduce_fusion
  384.3 6.9 pad_maximum_fusion.1
  391.2 7.0 pad_maximum_fusion.2
  398.2 54.9 %all-to-all-done = bf16[16,48,2560]{2,1,0:T(8,128)(2,1)} async-done(((bf16[16,48,2560]{2,1,0:T(8,128)(2,1)}), bf16[16,48,2560]{2,1,0:T(8,128)(2,1)}, u32[]{:S(2)}, u32[]{:S(2)}) %all-to-all-start) | async-done | bytes 3932192 | tf_op jit(solution)/shard_map/all_to_all | solution.py:70
  453.1 142.4 %while.11 = (s32[]{:T(128)}, bf16[20,768,128]{2,1,0:T(8,128)(2,1)}, pred[1536]{0:T(1024)(128)(4,1)S(1)}, s32[20]{0:T(128)S(1)}, bf16[768,2560]{1,0:T(8,128)(2,1)...) while((s32[]{:T(128)}, bf16[20,768,128]{2,1,0:T(8,128)(2,1)}, ...), condition=%wide.region_4.5_spmd, body=%wide.region_1.4_spmd.sunk | while | flops 617150976 | bytes 15357099 | solution.py:49
  457.4 2.8 fusion.47
  464.5 2.8 fusion.47
  478.8 2.8 fusion.47
  485.9 2.8 fusion.47
  493.0 2.8 fusion.47
  500.1 2.8 fusion.47
  507.3 2.8 fusion.47
  521.5 2.8 fusion.47
  528.6 2.8 fusion.47
  542.9 2.8 fusion.47
  550.0 2.8 fusion.47
  564.2 2.8 fusion.47
  571.4 2.8 fusion.47
  585.6 2.8 fusion.47
  592.7 2.8 fusion.47
  595.5 6.9 copy.7
  602.4 7.5 %reshape_reshape.3 = bf16[16,48,2560]{2,1,0:T(8,128)(2,1)} reshape(bf16[768,20,128]{2,1,0:T(8,128)(2,1)} %copy.7) | data formatting | bytes 7864320 | tf_op jit(solution)/shard_map/reshape;reshape | solution.py:95
  609.9 105.3 %all_to_all.32 = bf16[16,48,2560]{2,1,0:T(8,128)(2,1)S(1)} all-to-all(bf16[16,48,2560]{2,1,0:T(8,128)(2,1)} %reshape_reshape.3), channel_id=1, replica_groups=mesh['view'=2,'seq'=16] {'seq'}, dimensions={0} | all-to-all | bytes 7864320 | tf_op jit(solution)/shard_map/all_to_all | solution.py:94
  (80 shorter events, 90.7 us)
Async XLA Ops:
  0.0 83.3 %all-to-all-start.1 = ((bf16[16,48,2560]{2,1,0:T(8,128)(2,1)}), bf16[16,48,2560]{2,1,0:T(8,128)(2,1)}, u32[]{:S(2)}, u32[]{:S(2)}) async-start(bf16[16,48,2560]{2,1,0:T(8,128)(2,1)} %bitcast.69), calls=%async_computation.1 | async-start | bytes 7864320 | tf_op jit(solution)/shard_map/all_to_all | solution.py:73
  15.6 86.8 %collective-permute-start = (bf16[2,768,2560]{2,1,0:T(8,128)(2,1)}, bf16[2,768,2560]{2,1,0:T(8,128)(2,1)}, u32[]{:S(2)}, u32[]{:S(2)}) collective-permute-start(bf16[2,768,2560]{2,1,0:T(8,128)(2,1)} %pad_maximum_fusion), channel_id=1, source_target_pairs={{0,16},{16,0},{1,17},{17,1},{2,18},{18,2},{3,19},{19,3},{4,20},{20... | collective-permute-start | bytes 23592968 | tf_op jit(solution)/shard_map/ppermute | solution.py:12
  83.3 93.0 %all-to-all-start.3 = ((bf16[16,48,2560]{2,1,0:T(8,128)(2,1)}), bf16[16,48,2560]{2,1,0:T(8,128)(2,1)}, u32[]{:S(2)}, u32[]{:S(2)}) async-start(bf16[16,48,2560]{2,1,0:T(8,128)(2,1)} %bitcast.70), calls=%async_computation.3 | async-start | bytes 7864320 | tf_op jit(solution)/shard_map/all_to_all | solution.py:74
  176.3 106.7 %copy-start = (bf16[1,768,2560]{2,1,0:T(8,128)(2,1)S(1)}, bf16[1,768,2560]{2,1,0:T(8,128)(2,1)}, u32[]{:S(2)}) copy-start(bf16[1,768,2560]{2,1,0:T(8,128)(2,1)} %get-tuple-element.71) | copy-start | bytes 11796484
  374.6 5.4 copy-start.1
  374.6 78.5 %all-to-all-start = ((bf16[16,48,2560]{2,1,0:T(8,128)(2,1)}), bf16[16,48,2560]{2,1,0:T(8,128)(2,1)}, u32[]{:S(2)}, u32[]{:S(2)}) async-start(bf16[16,48,2560]{2,1,0:T(8,128)(2,1)} %bitcast.75), calls=%async_computation | async-start | bytes 7864320 | tf_op jit(solution)/shard_map/all_to_all | solution.py:70
where the time goes:
time: 719 us; the launch traced here: 717 us
  blocking collectives  304 us (42%)
  waiting for transfers between devices  191 us (27%)
  matrix products  96.2 us (13%)
  other arithmetic  45.7 us (6%)
  local copies, waits for them, and re-layouts  35.3 us (5%)
  starting transfers between devices  32.1 us (4%)
  loops' own time  12.6 us (2%)
    all_to_all x1, blocking collectives, per_device(): lax.all_to_all(other[0].reshape(shape_band), 'seq', split_axis=0, concat_...  107 us
    all_to_all x1, blocking collectives, per_device(): lax.all_to_all(shortened(mixed.reshape(shape_band)), 'seq', split_axis=0,...  105 us
    all_to_all x1, blocking collectives, per_device(): lax.all_to_all(other[1].reshape(shape_band), 'seq', split_axis=0, concat_...  91.6 us
    all_to_all x1, waiting for transfers between devices, per_device(): lax.all_to_all(values[0].reshape(shape_band), 'seq', split_axis=0, concat...  68.3 us
    all_to_all x1, waiting for transfers between devices, per_device(): lax.all_to_all(keys[0].reshape(shape_band), 'seq', split_axis=0, concat_a...  67.7 us
    dot_general x20, matrix products, one_head(): jnp.dot(weight.astype(jnp.bfloat16), vpart, preferred_element_type=jnp.fl...  55.8 us
    all_to_all x1, waiting for transfers between devices, per_device(): lax.all_to_all(query[0].reshape(shape_band), 'seq', split_axis=0, concat_...  54.9 us
    dot_general x20, matrix products, one_head(): lax.dot_general(qpart, kpart, (((1,), (1,)), ((), ())), preferred_element...  40.4 us
  transfers between devices with their start and end apart: 4, of which 3 were waited for; matrix products, arithmetic and copies ran while one was open for 4% of the time, Pallas kernels for 0%

commit v1 on v0

v1 whole, which is shorter than its diff:
```python
import functools

import jax
import jax.numpy as jnp
from jax import lax
from jax.experimental import pallas as pl
from jax.experimental.pallas import tpu as pltpu
from jax.sharding import PartitionSpec as P

HD = 128
KBLK = 128
GROUP_HEADS = 4
ROWS = 256
MESH = pl.DeviceIdType.MESH


def block_mask(listed, count, blocks, width):
    slots = jnp.arange(listed.shape[0], dtype=jnp.int32)
    hits = (listed[:, None] == jnp.arange(blocks, dtype=jnp.int32)[None, :]) & (slots < count)[
        :, None
    ]
    return jnp.repeat(jnp.any(hits, axis=0), width, total_repeat_length=blocks * width)


def attend_tile(q, near_k, near_v, far_k, far_v, bias):
    scale = HD**-0.5
    dims = (((1,), (1,)), ((), ()))
    near = lax.dot_general(q, near_k, dims, preferred_element_type=jnp.float32)
    far = lax.dot_general(q, far_k, dims, preferred_element_type=jnp.float32) + bias
    top = jnp.maximum(
        jnp.max(near, axis=1, keepdims=True), jnp.max(far, axis=1, keepdims=True)
    )
    near_w = jnp.exp((near - top) * scale)
    far_w = jnp.exp((far - top) * scale)
    total = jnp.sum(near_w, axis=1, keepdims=True) + jnp.sum(far_w, axis=1, keepdims=True)
    mixed = jnp.dot(near_w.astype(jnp.bfloat16), near_v, preferred_element_type=jnp.float32)
    mixed += jnp.dot(far_w.astype(jnp.bfloat16), far_v, preferred_element_type=jnp.float32)
    return (mixed / total).astype(jnp.bfloat16)


def wait_for(ref, sem):
    pltpu.make_async_copy(ref, ref, sem).wait()


def kernel(n, cells, q, k, v, bias, out, qb, kb, vb, fk, fv, ob,
           send, recv, far_send, far_recv, out_send, out_recv):
    me = lax.axis_index("seq")
    view = lax.axis_index("view")
    rows, feat = qb.shape
    width = GROUP_HEADS * HD if feat % (GROUP_HEADS * HD) == 0 else HD
    groups = feat // width
    tile = ROWS if rows % ROWS == 0 else rows

    def span(d):
        return pl.ds(pl.multiple_of(d * cells, cells), cells)

    def peer(i):
        return lax.rem(me + i, n)

    barrier = pltpu.get_barrier_semaphore()

    @pl.loop(1, n)
    def _(i):
        pl.semaphore_signal(barrier, inc=1, device_id=(view, peer(i)), device_id_type=MESH)

    pl.semaphore_signal(barrier, inc=1, device_id=(1 - view, me), device_id_type=MESH)
    pl.semaphore_wait(barrier, n)

    moved = ((q, qb), (k, kb), (v, vb))
    for g in range(groups):
        cols = pl.ds(g * width, width)
        for a, (src, dst) in enumerate(moved):
            pltpu.make_async_copy(
                src.at[span(me), cols], dst.at[span(me), cols], recv.at[g, a]
            ).start()

        @pl.loop(1, n)
        def _(i):
            d = peer(i)
            for a, (src, dst) in enumerate(moved):
                pltpu.make_async_remote_copy(
                    src_ref=src.at[span(d), cols],
                    dst_ref=dst.at[span(me), cols],
                    send_sem=send.at[g, a],
                    recv_sem=recv.at[g, a],
                    device_id=(view, d),
                    device_id_type=MESH,
                ).start()

    for g in range(groups):
        cols = pl.ds(g * width, width)
        far = []
        for a, (near, other) in enumerate(((kb, fk), (vb, fv))):
            wait_for(near.at[:, cols], recv.at[g, a + 1])
            copy = pltpu.make_async_remote_copy(
                src_ref=near.at[:, cols],
                dst_ref=other.at[:, cols],
                send_sem=far_send.at[g, a],
                recv_sem=far_recv.at[g, a],
                device_id=(1 - view, me),
                device_id_type=MESH,
            )
            copy.start()
            far.append(copy)
        wait_for(qb.at[:, cols], recv.at[g, 0])
        for copy in far:
            copy.wait()

        @pl.loop(0, width // HD)
        def _(h):
            col = pl.ds(pl.multiple_of(g * width + h * HD, HD), HD)
            near_k, near_v, far_k, far_v = kb[:, col], vb[:, col], fk[:, col], fv[:, col]
            for r in range(rows // tile):
                part = pl.ds(r * tile, tile)
                ob[part, col] = attend_tile(
                    qb[part, col], near_k, near_v, far_k, far_v, bias[...]
                )

        pltpu.make_async_copy(ob.at[span(me), cols], out.at[span(me), cols], out_recv).start()

        @pl.loop(1, n)
        def _(i):
            d = peer(i)
            pltpu.make_async_remote_copy(
                src_ref=ob.at[span(d), cols],
                dst_ref=out.at[span(me), cols],
                send_sem=out_send,
                recv_sem=out_recv,
                device_id=(view, d),
                device_id_type=MESH,
            ).start()

    sent = pl.ds(0, (n - 1) * cells)
    for g in range(groups):
        cols = pl.ds(g * width, width)
        for a, (src, _) in enumerate(moved):
            wait_for(src.at[sent, cols], send.at[g, a])
    wait_for(ob.at[sent, :], out_send)
    wait_for(out, out_recv)


def by_kernel(query, keys, values, live):
    n = lax.axis_size("seq")
    rows, feat = query.shape
    cells = rows // n
    bias = jnp.where(live, 0.0, -1e30).astype(jnp.float32)[None, :]
    width = GROUP_HEADS * HD if feat % (GROUP_HEADS * HD) == 0 else HD
    groups = feat // width
    anywhere = pl.BlockSpec(memory_space=pl.ANY)
    sems = pltpu.SemaphoreType.DMA
    return pl.pallas_call(
        functools.partial(kernel, n, cells),
        out_shape=jax.ShapeDtypeStruct((rows, feat), jnp.bfloat16),
        in_specs=[anywhere, anywhere, anywhere, pl.BlockSpec(memory_space=pltpu.VMEM)],
        out_specs=anywhere,
        scratch_shapes=[pltpu.VMEM((rows, feat), jnp.bfloat16)] * 6
        + [
            sems((groups, 3)),
            sems((groups, 3)),
            sems((groups, 2)),
            sems((groups, 2)),
            sems,
            sems,
        ],
        compiler_params=pltpu.CompilerParams(
            collective_id=0, has_side_effects=True, vmem_limit_bytes=56 * 1024 * 1024
        ),
    )(query, keys, values, bias)


def by_collectives(query, keys, values, live):
    n = lax.axis_size("seq")
    rows, feat = query.shape

    def swap(x):
        x = x.reshape(n, rows // n, feat)
        return lax.all_to_all(x, "seq", split_axis=0, concat_axis=0, tiled=True).reshape(rows, feat)

    def partner(x):
        return lax.ppermute(x, "view", [(0, 1), (1, 0)])

    band_k, band_v = swap(keys), swap(values)
    far_k, far_v = partner(band_k), partner(band_v)
    band_q = swap(query)
    bias = jnp.where(live, 0.0, -1e30).astype(jnp.float32)[None, :]

    def one_head(head):
        parts = [
            lax.dynamic_slice_in_dim(x, head * HD, HD, 1)
            for x in (band_q, band_k, band_v, far_k, far_v)
        ]
        return attend_tile(*parts, bias)

    outs = lax.map(one_head, jnp.arange(feat // HD, dtype=jnp.int32))
    return swap(jnp.transpose(outs, (1, 0, 2)).reshape(rows, feat))


def per_device(query, keys, values, block_list, block_count):
    rows = query.shape[1]
    blocks = rows // KBLK
    live = block_mask(block_list[0, 0], block_count[0, 0], blocks, KBLK)
    aligned = rows // lax.axis_size("seq") % 16 == 0
    run = by_kernel if aligned else by_collectives
    return run(query[0], keys[0], values[0], live)[None]


def solution(mesh):
    in_specs = (
        P("view", "seq", None),
        P("view", "seq", None),
        P("view", "seq", None),
        P("view", "seq", None),
        P("view", "seq"),
    )
    return jax.shard_map(
        per_device, mesh=mesh, in_specs=in_specs, out_specs=P("view", "seq", None), check_vma=False
    )
```

time: 719 us -> 364 us (0.51)
  Pallas kernels: 0 us -> 350 us
  blocking collectives: 304 us -> 0 us
  waiting for transfers between devices: 191 us -> 0 us
  matrix products: 96.2 us -> 0 us
  other arithmetic: 45.7 us -> 5.09 us
  starting transfers between devices: 32.1 us -> 0 us
  local copies, waits for them, and re-layouts: 35.3 us -> 4.97 us
  loops' own time: 12.6 us -> 0 us
    pallas_call x0 -> x1, Pallas kernels: none -> 350 us  [by_kernel(): pl.pallas_call(functools.partial(kernel, n, cells), out_shape=jax.ShapeDt...]
    all_to_all x3 -> x0, blocking collectives: 304 us -> none  [the longest x1 107 us: per_device(): lax.all_to_all(other[0].reshape(shape_band), 'seq', split_axis=0, concat_...]
    all_to_all x3 -> x0, waiting for transfers between devices: 191 us -> none  [the longest x1 68.3 us: per_device(): lax.all_to_all(values[0].reshape(shape_band), 'seq', split_axis=0, concat...]
    dot_general x40 -> x0, matrix products: 96.2 us -> none  [the longest x20 55.8 us: one_head(): jnp.dot(weight.astype(jnp.bfloat16), vpart, preferred_element_type=jnp.fl...]
    all_to_all x3 -> x0, starting transfers between devices: 32.1 us -> none  [the longest x1 19.1 us: per_device(): lax.all_to_all(values[0].reshape(shape_band), 'seq', split_axis=0, concat...]
    reduce_sum x20 -> x0, other arithmetic: 20.9 us -> none  [one_head(): total = jnp.sum(weight, axis=1, keepdims=True)]
    concatenate x2 -> x0, other arithmetic: 13.9 us -> none  [the longest x1 6.98 us: attend(): vals = jnp.concatenate((near_v, far_v), 0)]
    dynamic_slice x20 -> x0, local copies, waits for them, and re-layouts: 12.7 us -> none  [attend(): outs = lax.map(one_head, jnp.arange(HEADS, dtype=jnp.int32))]
  transfers between devices with their start and end apart: 4 -> 0, of which waited for: 3 -> 0; matrix products, arithmetic and copies ran while one was open for 4% -> 0% of each run, Pallas kernels for 0% -> 0%
where the time goes in v1:
time: 364 us; the launch traced here: 360 us
  Pallas kernels  350 us (96%)
  other arithmetic  5.09 us (1%)
  local copies, waits for them, and re-layouts  4.97 us (1%)
    pallas_call x1, Pallas kernels, by_kernel(): pl.pallas_call(functools.partial(kernel, n, cells), out_shape=jax.ShapeDt...  350 us

profile of v1, /device:TPU:0, one launch (start us, length us, event | category | flops | bytes accessed | tf_op | source)
XLA Modules:
  0.0 360.3 jit_solution(9078698646569285086)
XLA Ops:
  0.7 0.7 fusion.2
  1.4 0.7 fusion.3
  2.1 4.3 %fusion.bias = f32[1,768]{1,0:T(1,128)} fusion(pred[]{:T(512)} %bitcast.5, pred[]{:T(512)} %bitcast.6, pred[]{:T(512)} %bitcast.7, pred[]{:T(512)} %bitcast.8, pred[]{:T(512)} %bitcast.10, pred[]{:T(512)} %bitcast.9, s32[1,1,6,128]{3,2,1,0:T(8,128)S(1)} %get-tuple-element.23, s32[1,1,6,128]{3,2,1,0:T(8,128)S(1)} %get-tuple-element.24), kind=kLoop, calls=%fused_computation.3 | loop fusion | flops 14592 | bytes 9222 | tf_op jit(solution)/shard_map/jit(_where)/select_n | solution.py:146
  6.4 349.6 %shard_map.55 = bf16[768,2560]{1,0:T(8,128)(2,1)} custom-call(bf16[768,2560]{1,0:T(8,128)(2,1)} %bitcast.38, bf16[768,2560]{1,0:T(8,128)(2,1)} %bitcast.39, bf16[768,2560]{1,0:T(8,128)(2,1)} %bitcast.40, f32[1,768]{1,0:T(1,128)} %fusion.bias), custom_call_target="tpu_custom_call" | custom-call | tf_op jit(solution)/shard_map/pallas_call | solution.py:151
  356.0 4.3 %copy.14 = bf16[1,768,2560]{2,1,0:T(8,128)(2,1)} copy(bf16[1,768,2560]{2,1,0:T(8,128)(2,1)} %bitcast.37) | data formatting | bytes 7864320
  (2 shorter events, 0.0 us)

commit v2 on v1

--- a/solution.py
+++ b/solution.py
@@ -9,7 +9,8 @@
 
 HD = 128
 KBLK = 128
-GROUP_HEADS = 4
+GROUP_HEADS = 2
+LAST_HEADS = (1, 1)
 ROWS = 256
 MESH = pl.DeviceIdType.MESH
 
@@ -38,24 +39,35 @@
     return (mixed / total).astype(jnp.bfloat16)
 
 
+def head_groups(heads):
+    tail = LAST_HEADS if heads > sum(LAST_HEADS) else ()
+    left = heads - sum(tail)
+    sizes = [min(GROUP_HEADS, left - done) for done in range(0, left, GROUP_HEADS)]
+    groups, start = [], 0
+    for size in (*sizes, *tail):
+        groups.append((start, size))
+        start += size
+    return groups
+
+
 def wait_for(ref, sem):
     pltpu.make_async_copy(ref, ref, sem).wait()
 
 
-def kernel(n, cells, q, k, v, bias, out, qb, kb, vb, fk, fv, ob,
+def kernel(n, cells, q, k, v, listed, count, out, qb, kb, vb, fk, fv, ob, bias,
            send, recv, far_send, far_recv, out_send, out_recv):
     me = lax.axis_index("seq")
     view = lax.axis_index("view")
     rows, feat = qb.shape
-    width = GROUP_HEADS * HD if feat % (GROUP_HEADS * HD) == 0 else HD
-    groups = feat // width
+    groups = head_groups(feat // HD)
+    stride = n // 2 - 1 if n % 4 == 0 and n > 4 else 1
     tile = ROWS if rows % ROWS == 0 else rows
 
     def span(d):
         return pl.ds(pl.multiple_of(d * cells, cells), cells)
 
     def peer(i):
-        return lax.rem(me + i, n)
+        return lax.rem(me + i * stride, n)
 
     barrier = pltpu.get_barrier_semaphore()
 
@@ -67,8 +79,8 @@
     pl.semaphore_wait(barrier, n)
 
     moved = ((q, qb), (k, kb), (v, vb))
-    for g in range(groups):
-        cols = pl.ds(g * width, width)
+    for g, (first, size) in enumerate(groups):
+        cols = pl.ds(first * HD, size * HD)
         for a, (src, dst) in enumerate(moved):
             pltpu.make_async_copy(
                 src.at[span(me), cols], dst.at[span(me), cols], recv.at[g, a]
@@ -87,8 +99,15 @@
                     device_id_type=MESH,
                 ).start()
 
-    for g in range(groups):
-        cols = pl.ds(g * width, width)
+    token = lax.broadcasted_iota(jnp.int32, (1, rows), 1)
+    live = token < 0
+    for m in range(listed.shape[0]):
+        low = jnp.where(m < count[0], listed[m], -1) * KBLK
+        live |= (token >= low) & (token < low + KBLK)
+    bias[...] = jnp.where(live, 0.0, -1e30)
+
+    for g, (first, size) in enumerate(groups):
+        cols = pl.ds(first * HD, size * HD)
         far = []
         for a, (near, other) in enumerate(((kb, fk), (vb, fv))):
             wait_for(near.at[:, cols], recv.at[g, a + 1])
@@ -106,9 +125,9 @@
         for copy in far:
             copy.wait()
 
-        @pl.loop(0, width // HD)
+        @pl.loop(0, size)
         def _(h):
-            col = pl.ds(pl.multiple_of(g * width + h * HD, HD), HD)
+            col = pl.ds(pl.multiple_of((first + h) * HD, HD), HD)
             near_k, near_v, far_k, far_v = kb[:, col], vb[:, col], fk[:, col], fv[:, col]
             for r in range(rows // tile):
                 part = pl.ds(r * tile, tile)
@@ -131,30 +150,29 @@
             ).start()
 
     sent = pl.ds(0, (n - 1) * cells)
-    for g in range(groups):
-        cols = pl.ds(g * width, width)
+    for g, (first, size) in enumerate(groups):
+        cols = pl.ds(first * HD, size * HD)
         for a, (src, _) in enumerate(moved):
             wait_for(src.at[sent, cols], send.at[g, a])
     wait_for(ob.at[sent, :], out_send)
     wait_for(out, out_recv)
 
 
-def by_kernel(query, keys, values, live):
+def by_kernel(query, keys, values, listed, count):
     n = lax.axis_size("seq")
     rows, feat = query.shape
     cells = rows // n
-    bias = jnp.where(live, 0.0, -1e30).astype(jnp.float32)[None, :]
-    width = GROUP_HEADS * HD if feat % (GROUP_HEADS * HD) == 0 else HD
-    groups = feat // width
+    groups = len(head_groups(feat // HD))
     anywhere = pl.BlockSpec(memory_space=pl.ANY)
     sems = pltpu.SemaphoreType.DMA
     return pl.pallas_call(
         functools.partial(kernel, n, cells),
         out_shape=jax.ShapeDtypeStruct((rows, feat), jnp.bfloat16),
-        in_specs=[anywhere, anywhere, anywhere, pl.BlockSpec(memory_space=pltpu.VMEM)],
+        in_specs=[anywhere] * 3 + [pl.BlockSpec(memory_space=pltpu.SMEM)] * 2,
         out_specs=anywhere,
         scratch_shapes=[pltpu.VMEM((rows, feat), jnp.bfloat16)] * 6
         + [
+            pltpu.VMEM((1, rows), jnp.float32),
             sems((groups, 3)),
             sems((groups, 3)),
             sems((groups, 2)),
@@ -165,12 +183,13 @@
         compiler_params=pltpu.CompilerParams(
             collective_id=0, has_side_effects=True, vmem_limit_bytes=56 * 1024 * 1024
         ),
-    )(query, keys, values, bias)
-
-
-def by_collectives(query, keys, values, live):
+    )(query, keys, values, listed, count)
+
+
+def by_collectives(query, keys, values, listed, count):
     n = lax.axis_size("seq")
     rows, feat = query.shape
+    live = block_mask(listed, count[0], rows // KBLK, KBLK)
 
     def swap(x):
         x = x.reshape(n, rows // n, feat)
@@ -196,12 +215,9 @@
 
 
 def per_device(query, keys, values, block_list, block_count):
-    rows = query.shape[1]
-    blocks = rows // KBLK
-    live = block_mask(block_list[0, 0], block_count[0, 0], blocks, KBLK)
-    aligned = rows // lax.axis_size("seq") % 16 == 0
+    aligned = query.shape[1] // lax.axis_size("seq") % 16 == 0
     run = by_kernel if aligned else by_collectives
-    return run(query[0], keys[0], values[0], live)[None]
+    return run(query[0], keys[0], values[0], block_list[0, 0], block_count[0])[None]
 
 
 def solution(mesh):

time: 364 us -> 353 us (0.970); the launches traced: 360 us -> 353 us
  other arithmetic: 5.09 us -> 0 us
    select_n x1 -> x0, other arithmetic: 4.33 us -> none  [by_kernel(): bias = jnp.where(live, 0.0, -1e+30).astype(jnp.float32)[None, :]]
where the time goes in v2:
time: 353 us
  Pallas kernels  348 us (99%)
  local copies, waits for them, and re-layouts  4.29 us (1%)
    pallas_call x1, Pallas kernels, by_kernel(): pl.pallas_call(functools.partial(kernel, n, cells), out_shape=jax.ShapeDt...  348 us

profile of v2, /device:TPU:0, one launch (start us, length us, event | category | flops | bytes accessed | tf_op | source)
XLA Modules:
  0.0 353.1 jit_solution(12431167069473079642)
XLA Ops:
  0.7 348.2 %shard_map.55 = bf16[768,2560]{1,0:T(8,128)(2,1)} custom-call(bf16[768,2560]{1,0:T(8,128)(2,1)} %bitcast.8, bf16[768,2560]{1,0:T(8,128)(2,1)} %bitcast.9, bf16[768,2560]{1,0:T(8,128)(2,1)} %bitcast.10, s32[4]{0:T(128)} %bitcast.11, s32[1]{0:T(128)} %bitcast.6.count), custom_call_target="tpu_custom_call" | custom-call | tf_op jit(solution)/shard_map/pallas_call | solution.py:168
  348.8 4.3 %copy.8 = bf16[1,768,2560]{2,1,0:T(8,128)(2,1)} copy(bf16[1,768,2560]{2,1,0:T(8,128)(2,1)} %bitcast.7) | data formatting | bytes 7864320

commit v3 on v2

--- a/solution.py
+++ b/solution.py
@@ -78,7 +78,7 @@
     pl.semaphore_signal(barrier, inc=1, device_id=(1 - view, me), device_id_type=MESH)
     pl.semaphore_wait(barrier, n)
 
-    moved = ((q, qb), (k, kb), (v, vb))
+    moved = ((k, kb), (v, vb), (q, qb))
     for g, (first, size) in enumerate(groups):
         cols = pl.ds(first * HD, size * HD)
         for a, (src, dst) in enumerate(moved):
@@ -110,7 +110,7 @@
         cols = pl.ds(first * HD, size * HD)
         far = []
         for a, (near, other) in enumerate(((kb, fk), (vb, fv))):
-            wait_for(near.at[:, cols], recv.at[g, a + 1])
+            wait_for(near.at[:, cols], recv.at[g, a])
             copy = pltpu.make_async_remote_copy(
                 src_ref=near.at[:, cols],
                 dst_ref=other.at[:, cols],
@@ -121,7 +121,7 @@
             )
             copy.start()
             far.append(copy)
-        wait_for(qb.at[:, cols], recv.at[g, 0])
+        wait_for(qb.at[:, cols], recv.at[g, 2])
         for copy in far:
             copy.wait()
 

time: 353 us -> 353 us (level)
  no operation moved by 1% of the time
where the time goes in v3:
time: 353 us
  Pallas kernels  348 us (99%)
  local copies, waits for them, and re-layouts  4.29 us (1%)
    pallas_call x1, Pallas kernels, by_kernel(): pl.pallas_call(functools.partial(kernel, n, cells), out_shape=jax.ShapeDt...  348 us

profile of v3, /device:TPU:0, one launch (start us, length us, event | category | flops | bytes accessed | tf_op | source)
XLA Modules:
  0.0 353.3 jit_solution(723721813845798685)
XLA Ops:
  0.7 348.3 %shard_map.55 = bf16[768,2560]{1,0:T(8,128)(2,1)} custom-call(bf16[768,2560]{1,0:T(8,128)(2,1)} %bitcast.8, bf16[768,2560]{1,0:T(8,128)(2,1)} %bitcast.9, bf16[768,2560]{1,0:T(8,128)(2,1)} %bitcast.10, s32[4]{0:T(128)} %bitcast.11, s32[1]{0:T(128)} %bitcast.6.count), custom_call_target="tpu_custom_call" | custom-call | tf_op jit(solution)/shard_map/pallas_call | solution.py:168
  349.0 4.3 %copy.8 = bf16[1,768,2560]{2,1,0:T(8,128)(2,1)} copy(bf16[1,768,2560]{2,1,0:T(8,128)(2,1)} %bitcast.7) | data formatting | bytes 7864320
